TPU v7x, 32 devices: a whole 2x2x4 slice. The times are simulated.
32 devices in a mesh: crow: 2 (over y), ccol: 8 (over z, x), half: 2 (over core).
Axes of the slice: x: 2, y: 2, z: 4, core: 2. Of those that a mesh axis runs over, the one named last changes fastest.
Arguments:
- operator: bfloat16 [2, 8, 2048, 2048], P('crow', 'ccol', 'half'), may hold values from -0.09375 to 0.09375
- east_sources: bfloat16 [2, 8, 384, 2048], P('crow', 'ccol', None, 'half'), may hold values from -6 to 6
- west_sources: bfloat16 [2, 8, 384, 2048], P('crow', 'ccol', None, 'half'), may hold values from -6 to 6
Outputs:
- east_traces: bfloat16 [2, 8, 384, 2048], P('crow', 'ccol', None, 'half')
- west_traces: bfloat16 [2, 8, 384, 2048], P('crow', 'ccol', None, 'half')
All inputs are finite; a program needn't handle non-finite values.
Results may differ from a plain program's by a relative error of at most 0.025.
Values may be sent and summed in bfloat16 or wider, within the bound.
A program may use at most 64 MiB of HBM per device.

v0:
```python
import functools

import jax
import jax.numpy as jnp
from jax import lax
from jax.experimental import pallas as pl
from jax.experimental.pallas import tpu as pltpu
from jax.sharding import PartitionSpec as P

BLOCKS = 12
PIECES = 4
CHUNK = 256
TILE = 256
DIRECT = 1
RELAY_AT = 9
MESH = pl.DeviceIdType.MESH


def sweeps(rows, cols, op_ref, es_ref, ws_ref, eo_ref, wo_ref,
           mats, src, from_row, from_col, relay, out, acc,
           op_sem, src_sem, row_sem, col_sem, relay_sem, out_sem, send_sem, keep_sem):
    row, col, half = lax.axis_index("crow"), lax.axis_index("ccol"), lax.axis_index("half")
    blocks, block_rows, width = es_ref.shape
    pieces, piece = from_col.shape[1], from_col.shape[3]
    mine = pieces // 2
    chunks, chunk, full = mats.shape[1:]
    own_chunks = chunks // 2
    per_piece = piece // chunk

    fwd = half == 0
    step = 1 - 2 * half
    last = cols - 1
    e_level = row + col
    w_level = rows - 1 - row + last - col
    level = jnp.where(fwd, e_level, w_level)
    e_first, w_first = e_level == 0, w_level == 0
    has_n, has_s, has_w, has_e = row > 0, row < rows - 1, col > 0, col < last
    up_row, dn_row = (fwd & has_n) | (~fwd & has_s), (fwd & has_s) | (~fwd & has_n)
    up_col, dn_col = (fwd & has_w) | (~fwd & has_e), (fwd & has_e) | (~fwd & has_w)
    next_row, next_col = {"crow": row + step}, {"ccol": col + step}
    other = {"half": 1 - half}

    mid = cols // 2
    detour = mid >= 2 and DIRECT < blocks
    src_col = mid - 1 + half
    via_col = half * last
    dst_col = mid - half
    is_src, is_via, is_dst = col == src_col, col == via_col, col == dst_col

    def local(a, b, sem):
        return pltpu.make_async_copy(a, b, sem)

    def remote(a, b, send, recv, who):
        return pltpu.make_async_remote_copy(
            src_ref=a, dst_ref=b, send_sem=send, recv_sem=recv, device_id=who, device_id_type=MESH)

    barrier = pltpu.get_barrier_semaphore()

    def greet(who):
        pl.semaphore_signal(barrier, inc=1, device_id=who, device_id_type=MESH)

    greet(other)
    for there, who in ((has_n, {"crow": row - 1}), (has_s, {"crow": row + 1}),
                       (has_w, {"ccol": col - 1}), (has_e, {"ccol": col + 1})):
        @pl.when(there)
        def _():
            for h in range(2):
                greet({**who, "half": h})
    count = 1 + 2 * (has_n.astype(jnp.int32) + has_s.astype(jnp.int32)
                     + has_w.astype(jnp.int32) + has_e.astype(jnp.int32))
    if detour:
        for there, whos in ((is_src, (via_col,)), (is_via, (src_col, dst_col)), (is_dst, (via_col,))):
            @pl.when(there)
            def _():
                for who in whos:
                    greet({"ccol": who})
        count += is_src.astype(jnp.int32) + 2 * is_via.astype(jnp.int32) + is_dst.astype(jnp.int32)

    def op_own(c):
        return local(op_ref.at[pl.ds(c * chunk, chunk)], mats.at[0, half * own_chunks + c],
                     op_sem.at[half * own_chunks + c])

    def op_give(c):
        return remote(op_ref.at[pl.ds(c * chunk, chunk)], mats.at[0, half * own_chunks + c],
                      send_sem.at[0], op_sem.at[half * own_chunks + c], other)

    def op_wait(c):
        local(op_ref.at[pl.ds(0, chunk)], mats.at[0, c], op_sem.at[c]).wait()

    def src_own(ref, q):
        p = half * mine + q
        return local(ref.at[:, :, q * piece:(q + 1) * piece], src.at[p], src_sem.at[p])

    def src_give(ref, q):
        p = half * mine + q
        return remote(ref.at[:, :, q * piece:(q + 1) * piece], src.at[p], send_sem.at[1], src_sem.at[p], other)

    def first_to(ref, k, q, buffer, sem, send, who):
        p = half * mine + q
        return remote(ref.at[k, :, q * piece:(q + 1) * piece], buffer.at[k, p], send_sem.at[send], sem.at[k, p], who)

    def firsts(ref, k, shift, h):
        return [copy for q in range(mine) for copy in (
            first_to(ref, k, q, from_col, col_sem, 2, {"ccol": col + shift, "half": h}),
            first_to(ref, k, q, from_row, row_sem, 3, {"crow": row + shift, "half": h}))]

    @pl.when(~(e_first | w_first))
    def _():
        for c in range(own_chunks):
            op_own(c).start()
    pl.semaphore_wait(barrier, count)

    for there, ref, trace, shift, h in ((e_first, es_ref, eo_ref, 1, 0), (w_first, ws_ref, wo_ref, -1, 1)):
        @pl.when(there)
        def _():
            @pl.loop(0, blocks)
            def _(k):
                for copy in firsts(ref, k, shift, h):
                    copy.start()
            local(ref, trace, keep_sem.at[h]).start()

    for c in range(own_chunks):
        op_give(c).start()

    @pl.when(e_first | w_first)
    def _():
        for c in range(own_chunks):
            op_own(c).start()

    @pl.when(fwd)
    def _():
        for q in range(mine):
            src_own(es_ref, q).start()
            src_give(ws_ref, q).start()

    @pl.when(~fwd)
    def _():
        for q in range(mine):
            src_own(ws_ref, q).start()
            src_give(es_ref, q).start()

    for there, buffer in ((up_row, from_row), (up_col, from_col)):
        @pl.when(~there)
        def _():
            @pl.loop(0, blocks)
            def _(k):
                buffer[k] = jnp.zeros(buffer.shape[1:], buffer.dtype)

    @pl.loop(0, chunks)
    def _(c):
        op_wait(c)

        @pl.when(fwd & (level > 0))
        def _():
            at = pl.multiple_of(c * chunk, chunk)
            for n in range(chunks):
                mats[1, n, :, pl.ds(at, chunk)] = mats[0, c, :, n * chunk:(n + 1) * chunk].T
    for p in range(pieces):
        local(es_ref.at[:, :, :piece], src.at[p], src_sem.at[p]).wait()

    use = 1 - half

    def to_row(k, p):
        return remote(out.at[k, p], from_row.at[k, p], send_sem.at[3], row_sem.at[k, p], next_row)

    def to_col(k, p):
        return remote(out.at[k, p], from_col.at[k, p], send_sem.at[2], col_sem.at[k, p], next_col)

    def to_via(k, p):
        return remote(out.at[k, p], relay.at[k, p], send_sem.at[2], relay_sem.at[k, p], {"ccol": via_col})

    def from_via(k, p):
        return remote(relay.at[k, p], from_col.at[k, p], send_sem.at[4], col_sem.at[k, p], {"ccol": dst_col})

    def keep(trace, k, p):
        return local(out.at[k, p], trace.at[k, :, (p % mine) * piece:(p % mine + 1) * piece], keep_sem.at[half])

    def give(trace, k, p):
        return remote(out.at[k, p], trace.at[k, :, (p % mine) * piece:(p % mine + 1) * piece],
                      send_sem.at[5], out_sem.at[0], other)

    def send(k, p):
        far = is_src & (k >= DIRECT)
        if detour:
            @pl.when(far)
            def _():
                to_via(k, p).start()

            @pl.when(dn_col & ~far)
            def _():
                to_col(k, p).start()
        else:
            @pl.when(dn_col)
            def _():
                to_col(k, p).start()

        @pl.when(dn_row)
        def _():
            to_row(k, p).start()

        @pl.when(fwd)
        def _():
            (keep if p < mine else give)(eo_ref, k, p).start()

        @pl.when(~fwd)
        def _():
            (give if p < mine else keep)(wo_ref, k, p).start()

    @pl.loop(0, blocks + (RELAY_AT if detour else 0))
    def _(s):
        if detour:
            j = s - RELAY_AT

            @pl.when(is_via & (j >= DIRECT))
            def _():
                for p in range(pieces):
                    to_via(j, p).wait_recv()
                    from_via(j, p).start()

        @pl.when((level > 0) & (s < blocks))
        def _():
            for p in range(pieces):
                @pl.when(up_row)
                def _():
                    to_row(s, p).wait_recv()

                @pl.when(up_col)
                def _():
                    to_col(s, p).wait_recv()
                x = (from_row[s, p].astype(jnp.float32) + from_col[s, p].astype(jnp.float32)).astype(jnp.bfloat16)
                for n in range(0, full, TILE):
                    weights = mats[use, p * per_piece:(p + 1) * per_piece, :, n:n + TILE].reshape(piece, TILE)
                    part = jnp.dot(x, weights, preferred_element_type=jnp.float32)
                    o, at = n // piece, n % piece
                    if p == 0:
                        acc[:, n:n + TILE] = part + src[o, s, :, at:at + TILE].astype(jnp.float32)
                    elif p < pieces - 1:
                        acc[:, n:n + TILE] += part
                    else:
                        out[s, o, :, at:at + TILE] = (acc[:, n:n + TILE] + part).astype(jnp.bfloat16)
                        if n + TILE in (piece, full):
                            for ready in range(0 if n < piece else 1, o + 1):
                                send(s, ready)

    for c in range(own_chunks):
        op_give(c).wait_send()
    for q in range(mine):
        src_give(es_ref, q).wait_send()
    for there, ref, trace, shift, h in ((e_first, es_ref, eo_ref, 1, 0), (w_first, ws_ref, wo_ref, -1, 1)):
        @pl.when(there)
        def _():
            @pl.loop(0, blocks)
            def _(k):
                for copy in firsts(ref, k, shift, h):
                    copy.wait_send()
            local(ref, trace, keep_sem.at[h]).wait()

    @pl.when(level > 0)
    def _():
        @pl.when(dn_row)
        def _():
            remote(out, from_row, send_sem.at[3], row_sem.at[0, 0], next_row).wait_send()

        @pl.when(dn_col)
        def _():
            remote(out, from_col, send_sem.at[2], col_sem.at[0, 0], next_col).wait_send()
        local(eo_ref, eo_ref, keep_sem.at[half]).wait()
        remote(eo_ref, eo_ref, send_sem.at[5], out_sem.at[0], other).wait_send()
    if detour:
        @pl.when(is_via)
        def _():
            some = pl.ds(DIRECT, blocks - DIRECT)
            remote(relay.at[some], from_col.at[some], send_sem.at[4], col_sem.at[0, 0], {"ccol": dst_col}).wait_send()

    @pl.when((fwd & ~w_first) | (~fwd & ~e_first))
    def _():
        remote(eo_ref, eo_ref, send_sem.at[5], out_sem.at[0], other).wait_recv()


def local(rows, cols, operator, east_sources, west_sources):
    matrix = operator[0, 0]
    batch, width = east_sources.shape[2:]
    blocks, block_rows = BLOCKS, batch // BLOCKS
    cut = (blocks, block_rows, width)
    full = 2 * width
    piece = full // PIECES
    trace = pltpu.VMEM((blocks, PIECES, block_rows, piece), jnp.bfloat16)
    dma = pltpu.SemaphoreType.DMA
    hbm = functools.partial(pltpu.with_memory_space_constraint, memory_space=pltpu.HBM)
    east, west = pl.pallas_call(
        functools.partial(sweeps, rows, cols),
        out_shape=[jax.ShapeDtypeStruct(cut, jnp.bfloat16)] * 2,
        in_specs=[pl.BlockSpec(memory_space=pltpu.HBM)] * 3,
        out_specs=[pl.BlockSpec(memory_space=pltpu.VMEM)] * 2,
        scratch_shapes=[
            pltpu.VMEM((2, full // CHUNK, CHUNK, full), jnp.bfloat16),
            pltpu.VMEM((PIECES, blocks, block_rows, piece), jnp.bfloat16),
            trace, trace, trace, trace,
            pltpu.VMEM((block_rows, full), jnp.float32),
            dma((full // CHUNK,)), dma((PIECES,)),
            dma((blocks, PIECES)), dma((blocks, PIECES)), dma((blocks, PIECES)),
            dma((1,)), dma((6,)), dma((2,)),
        ],
        compiler_params=pltpu.CompilerParams(
            collective_id=0, has_side_effects=True, vmem_limit_bytes=32 * 2**20),
        name="sweeps",
    )(hbm(matrix), hbm(east_sources.reshape(cut)), hbm(west_sources.reshape(cut)))
    return east.reshape(1, 1, batch, width), west.reshape(1, 1, batch, width)


def solution(mesh):
    in_specs = (
        P("crow", "ccol", "half", None),
        P("crow", "ccol", None, "half"),
        P("crow", "ccol", None, "half"),
    )
    out_specs = (P("crow", "ccol", None, "half"), P("crow", "ccol", None, "half"))
    body = functools.partial(local, mesh.shape["crow"], mesh.shape["ccol"])
    return jax.shard_map(body, mesh=mesh, in_specs=in_specs, out_specs=out_specs, check_vma=False)
```

profile of v0, /device:TPU:0, one launch (start us, length us, event | category | flops | bytes accessed | tf_op | source)
XLA Modules:
  0.0 77.6 jit_solution(16223707810147546962)
XLA Ops:
  0.6 75.2 %sweeps.1 = (bf16[12,32,1024]{2,1,0:T(8,128)(2,1)S(1)}, bf16[12,32,1024]{2,1,0:T(8,128)(2,1)S(1)}) custom-call(bf16[1024,2048]{1,0:T(8,128)(2,1)} %bitcast.7, bf16[12,32,1024]{2,1,0:T(8,128)(2,1)} %bitcast.8, bf16[12,32,1024]{2,1,0:T(8,128)(2,1)} %bitcast.9), custom_call_target="tpu_custom_call" | custom-call | tf_op jit(solution)/shard_map/sweeps/pallas_call | solution.py:290
  75.9 0.9 %copy.7 = bf16[1,1,384,1024]{3,2,1,0:T(8,128)(2,1)} copy(bf16[1,1,384,1024]{3,2,1,0:T(8,128)(2,1)S(1)} %bitcast.6) | data formatting | bytes 1572864
  76.7 0.9 %copy.8 = bf16[1,1,384,1024]{3,2,1,0:T(8,128)(2,1)} copy(bf16[1,1,384,1024]{3,2,1,0:T(8,128)(2,1)S(1)} %bitcast.5) | data formatting | bytes 1572864
where the time goes:
time: 77.8 us; the launch traced here: 77.6 us
  Pallas kernels  75.2 us (97%)
  local copies, waits for them, and re-layouts  1.76 us (2%)
    pallas_call x1, Pallas kernels, local(): pl.pallas_call(functools.partial(sweeps, rows, cols), out_shape=[jax.Shap...  75.2 us
    unnamed x2, local copies, waits for them, and re-layouts  1.76 us

commit v1 on v0

v1 whole, which is shorter than its diff:
```python
import functools

import jax
import jax.numpy as jnp
from jax import lax
from jax.experimental import pallas as pl
from jax.experimental.pallas import tpu as pltpu
from jax.sharding import PartitionSpec as P

BLOCKS = 12
PIECES = 4
CHUNK = 256
TILE = 256
NEAR_LEAD, NEAR_REST = ((12, 12, 4), (12, 12, 4), (12, 12, 4)), ((8, 12, 4), (12, 12, 4), (12, 12, 4))
LONG_LEAD, LONG_REST = (0, 9), (1, 6)
NEAR_OFF, BACK_OFF, AHEAD_OFF = 4, 8, -7
MESH = pl.DeviceIdType.MESH


def sweeps(rows, cols, op_ref, es_ref, ws_ref, eo_ref, wo_ref,
           mats, src, from_row, inbox, out, acc, zeros,
           op_sem, src_sem, row_sem, col_sem, out_sem, send_sem, keep_sem):
    row, col, half = lax.axis_index("crow"), lax.axis_index("ccol"), lax.axis_index("half")
    blocks, block_rows, width = es_ref.shape
    pieces, piece = from_row.shape[1], from_row.shape[3]
    mine = pieces // 2
    chunks, chunk, full = mats.shape[1:]
    own_chunks = chunks // 2
    per_piece = piece // chunk

    fwd = half == 0
    step = 1 - 2 * half
    last = cols - 1
    e_level = row + col
    w_level = rows - 1 - row + last - col
    level = jnp.where(fwd, e_level, w_level)
    e_first, w_first = e_level == 0, w_level == 0
    has_n, has_s, has_w, has_e = row > 0, row < rows - 1, col > 0, col < last
    up_row, dn_row = (fwd & has_n) | (~fwd & has_s), (fwd & has_s) | (~fwd & has_n)
    up_col, dn_col = (fwd & has_w) | (~fwd & has_e), (fwd & has_e) | (~fwd & has_w)
    next_row, next_col = {"crow": row + step}, {"ccol": col + step}
    other = {"half": 1 - half}

    place = jnp.where(fwd, col, last - col)
    lead = jnp.where(fwd, row == 0, row == rows - 1)
    turns = (cols - 1) // 2
    detour = turns > 0
    middle = 2 * (turns // 2) + 1
    odd = place % 2 == 1
    def pick(cases, default):
        for cond, value in cases:
            default = jnp.where(cond, value, default)
        return default

    def at(where_to):
        return {"ccol": jnp.where(fwd, where_to, last - where_to)}

    def near_of(turn):
        kind = pick(((turn < turns // 2, 0), (turn == turns // 2, 1)), 2)
        values = [pick([(lead & (kind == i), NEAR_LEAD[i][v]) for i in range(3)]
                       + [(~lead & (kind == i), NEAR_REST[i][v]) for i in range(3)], 0) for v in range(3)]
        return jnp.minimum(values[0], blocks), jnp.minimum(values[1], blocks), values[2]

    def long_of():
        first, end = (pick(((lead, LONG_LEAD[v]),), LONG_REST[v]) for v in range(2))
        return jnp.minimum(first, blocks), jnp.minimum(end, blocks)

    can_near = odd & (place < last)
    can_long = (place == middle) & (lead | (middle + 3 <= last))
    near_first, near_end, near_pieces = near_of(place // 2)
    long_first, long_end = long_of()
    long_place = jnp.where(lead, 0, middle + 3)
    is_near = ~odd & (place + 2 <= last)
    is_long = (place == long_place) & (middle + 1 <= last)
    to_near = ~odd & (place >= 2)
    to_long = (place == middle + 1) & (long_place <= last)

    def local(a, b, sem):
        return pltpu.make_async_copy(a, b, sem)

    def remote(a, b, send, recv, who):
        return pltpu.make_async_remote_copy(
            src_ref=a, dst_ref=b, send_sem=send, recv_sem=recv, device_id=who, device_id_type=MESH)

    zeros[...] = jnp.zeros_like(zeros)
    barrier = pltpu.get_barrier_semaphore()

    def greet(who):
        pl.semaphore_signal(barrier, inc=1, device_id=who, device_id_type=MESH)

    greet(other)
    for there, who in ((has_n, {"crow": row - 1}), (has_s, {"crow": row + 1}),
                       (has_w, {"ccol": col - 1}), (has_e, {"ccol": col + 1})):
        @pl.when(there)
        def _():
            for h in range(2):
                greet({**who, "half": h})
    count = 1 + 2 * (has_n.astype(jnp.int32) + has_s.astype(jnp.int32)
                     + has_w.astype(jnp.int32) + has_e.astype(jnp.int32))
    if detour:
        for there, whos in ((can_near, (place - 1,)), (is_near, (place + 1, place + 2)), (to_near, (place - 2,)),
                            (can_long, (long_place,)), (is_long, (middle, middle + 1)), (to_long, (long_place,))):
            @pl.when(there)
            def _():
                for who in whos:
                    greet(at(who))
            count += len(whos) * there.astype(jnp.int32)

    def op_own(c):
        return local(op_ref.at[pl.ds(c * chunk, chunk)], mats.at[0, half * own_chunks + c],
                     op_sem.at[half * own_chunks + c])

    def op_give(c):
        return remote(op_ref.at[pl.ds(c * chunk, chunk)], mats.at[0, half * own_chunks + c],
                      send_sem.at[0], op_sem.at[half * own_chunks + c], other)

    def op_wait(c):
        local(op_ref.at[pl.ds(0, chunk)], mats.at[0, c], op_sem.at[c]).wait()

    def src_own(ref, q):
        p = half * mine + q
        return local(ref.at[:, :, q * piece:(q + 1) * piece], src.at[p], src_sem.at[p])

    def src_give(ref, q):
        p = half * mine + q
        return remote(ref.at[:, :, q * piece:(q + 1) * piece], src.at[p], send_sem.at[1], src_sem.at[p], other)

    def first_to(ref, k, q, buffer, sem, send, who):
        p = half * mine + q
        return remote(ref.at[k, :, q * piece:(q + 1) * piece], buffer.at[k, p], send_sem.at[send], sem.at[k, p], who)

    def firsts(ref, k, shift, h):
        return [copy for q in range(mine) for copy in (
            first_to(ref, k, q, inbox.at[0], col_sem.at[0], 2, {"ccol": col + shift, "half": h}),
            first_to(ref, k, q, from_row, row_sem, 3, {"crow": row + shift, "half": h}))]

    @pl.when(~(e_first | w_first))
    def _():
        for c in range(own_chunks):
            op_own(c).start()
    pl.semaphore_wait(barrier, count)

    for there, ref, trace, shift, h in ((e_first, es_ref, eo_ref, 1, 0), (w_first, ws_ref, wo_ref, -1, 1)):
        @pl.when(there)
        def _():
            @pl.loop(0, blocks)
            def _(k):
                for copy in firsts(ref, k, shift, h):
                    copy.start()
            local(ref, trace, keep_sem.at[h]).start()

    for c in range(own_chunks):
        op_give(c).start()

    @pl.when(e_first | w_first)
    def _():
        for c in range(own_chunks):
            op_own(c).start()

    @pl.when(fwd)
    def _():
        for q in range(mine):
            src_own(es_ref, q).start()
            src_give(ws_ref, q).start()

    @pl.when(~fwd)
    def _():
        for q in range(mine):
            src_own(ws_ref, q).start()
            src_give(es_ref, q).start()

    share = pl.cdiv(blocks, chunks)

    @pl.loop(0, chunks)
    def _(c):
        for there, buffer, sem in ((up_row, from_row, row_sem), (up_col, inbox.at[0], col_sem.at[0])):
            @pl.when((level > 0) & ~there)
            def _():
                @pl.loop(jnp.minimum(c * share, blocks), jnp.minimum(c * share + share, blocks))
                def _(k):
                    for p in range(pieces):
                        local(zeros, buffer.at[k, p], sem.at[k, p]).start()
        op_wait(c)

        @pl.when(fwd & (level > 0))
        def _():
            at = pl.multiple_of(c * chunk, chunk)
            for n in range(chunks):
                mats[1, n, :, pl.ds(at, chunk)] = mats[0, c, :, n * chunk:(n + 1) * chunk].T
    for p in range(pieces):
        local(es_ref.at[:, :, :piece], src.at[p], src_sem.at[p]).wait()

    use = 1 - half

    def to_row(k, p):
        return remote(out.at[k, p], from_row.at[k, p], send_sem.at[3], row_sem.at[k, p], next_row)

    def to_col(k, p):
        by_near = can_near & (k >= near_first) & (k < near_end) & (p < near_pieces)
        by_long = can_long & (k >= long_first) & (k < long_end)
        box = pick(((by_long, 2), (by_near, 1)), 0)
        who = at(pick(((by_long, long_place), (by_near, place - 1)), place + 1))
        return remote(out.at[k, p], inbox.at[box, k, p], send_sem.at[2], col_sem.at[box, k, p], who)

    def col_in(k, p):
        return local(zeros, inbox.at[0, k, p], col_sem.at[0, k, p])

    def row_in(k, p):
        return local(zeros, from_row.at[k, p], row_sem.at[k, p])

    def via_in(box, k, p):
        return local(zeros, inbox.at[box, k, p], col_sem.at[box, k, p])

    def pass_on(box, k, p):
        return remote(inbox.at[box, k, p], inbox.at[0, k, p], send_sem.at[4], col_sem.at[0, k, p],
                      at(place + 2 if box == 1 else middle + 1))

    def keep(trace, k, p):
        return local(out.at[k, p], trace.at[k, :, (p % mine) * piece:(p % mine + 1) * piece], keep_sem.at[half])

    def give(trace, k, p):
        return remote(out.at[k, p], trace.at[k, :, (p % mine) * piece:(p % mine + 1) * piece],
                      send_sem.at[5], out_sem.at[0], other)

    def send(k, some):
        @pl.when(dn_col)
        def _():
            for p in some:
                to_col(k, p).start()

        @pl.when(dn_row)
        def _():
            for p in some:
                to_row(k, p).start()

    def own(s, p):
        row_in(s, p).wait()
        col_in(s, p).wait()
        x = (from_row[s, p].astype(jnp.float32) + inbox[0, s, p].astype(jnp.float32)).astype(jnp.bfloat16)
        for n in range(0, full, TILE):
            weights = mats[use, p * per_piece:(p + 1) * per_piece, :, n:n + TILE].reshape(piece, TILE)
            part = jnp.dot(x, weights, preferred_element_type=jnp.float32)
            o, at = n // piece, n % piece
            if p == 0:
                acc[:, n:n + TILE] = part + src[o, s, :, at:at + TILE].astype(jnp.float32)
            elif p < pieces - 1:
                acc[:, n:n + TILE] += part
            else:
                out[s, o, :, at:at + TILE] = (acc[:, n:n + TILE] + part).astype(jnp.bfloat16)
                if n + TILE == piece:
                    send(s, (0,))
                if n + TILE == full:
                    send(s, range(1, pieces))

    def store(s):
        @pl.when(fwd)
        def _():
            for p in range(pieces):
                (keep if p < mine else give)(eo_ref, s, p).start()

        @pl.when(~fwd)
        def _():
            for p in range(pieces):
                (give if p < mine else keep)(wo_ref, s, p).start()

    hop_first, hop_end, hop_pieces = near_of(place // 2)
    long_off = jnp.where(lead, BACK_OFF, AHEAD_OFF)
    is_via = is_near & (hop_end > hop_first) | is_long & (long_end > long_first)

    def relay(t):
        @pl.when(is_via)
        def _():
            k = t - NEAR_OFF

            @pl.when(is_near & (k >= hop_first) & (k < hop_end))
            def _():
                @pl.loop(0, hop_pieces)
                def _(p):
                    via_in(1, k, p).wait()
                    pass_on(1, k, p).start()
            m = t - long_off

            @pl.when(is_long & (m >= long_first) & (m < long_end))
            def _():
                for p in range(pieces):
                    via_in(2, m, p).wait()
                    pass_on(2, m, p).start()

    if detour:
        @pl.loop(min(AHEAD_OFF, 0), 0)
        def _(t):
            relay(t)

    @pl.when(level > 0)
    def _():
        @pl.loop(0, blocks)
        def _(s):
            for p in range(pieces):
                own(s, p)
            store(s)
            if detour:
                relay(s)

    if detour:
        @pl.loop(jnp.where(level > 0, blocks, 0), blocks + max(NEAR_OFF, BACK_OFF))
        def _(t):
            relay(t)

    for c in range(own_chunks):
        op_give(c).wait_send()
    for q in range(mine):
        src_give(es_ref, q).wait_send()
    for there, ref, trace, shift, h in ((e_first, es_ref, eo_ref, 1, 0), (w_first, ws_ref, wo_ref, -1, 1)):
        @pl.when(there)
        def _():
            @pl.loop(0, blocks)
            def _(k):
                for copy in firsts(ref, k, shift, h):
                    copy.wait_send()
            local(ref, trace, keep_sem.at[h]).wait()

    @pl.when(level > 0)
    def _():
        @pl.when(dn_row)
        def _():
            remote(out, from_row, send_sem.at[3], row_sem.at[0, 0], next_row).wait_send()

        @pl.when(dn_col)
        def _():
            remote(out, from_row, send_sem.at[2], row_sem.at[0, 0], next_col).wait_send()
        local(eo_ref, eo_ref, keep_sem.at[half]).wait()
        remote(eo_ref, eo_ref, send_sem.at[5], out_sem.at[0], other).wait_send()
    if detour:
        for there, box, first, end, some in ((is_near, 1, hop_first, hop_end, hop_pieces),
                                             (is_long, 2, long_first, long_end, pieces)):
            @pl.when(there)
            def _():
                @pl.loop(first, end)
                def _(k):
                    @pl.loop(0, some)
                    def _(p):
                        pass_on(box, k, p).wait_send()

    @pl.when((fwd & ~w_first) | (~fwd & ~e_first))
    def _():
        remote(eo_ref, eo_ref, send_sem.at[5], out_sem.at[0], other).wait_recv()


def flush(east, west, east_out, west_out, sem):
    copies = [pltpu.make_async_copy(a, b, sem.at[i])
              for i, (a, b) in enumerate(((east, east_out), (west, west_out)))]
    for copy in copies:
        copy.start()
    for copy in copies:
        copy.wait()


def local(rows, cols, operator, east_sources, west_sources):
    matrix = operator[0, 0]
    batch, width = east_sources.shape[2:]
    blocks, block_rows = BLOCKS, batch // BLOCKS
    cut = (blocks, block_rows, width)
    full = 2 * width
    piece = full // PIECES
    cells = (blocks, PIECES, block_rows, piece)
    trace = pltpu.VMEM(cells, jnp.bfloat16)
    dma = pltpu.SemaphoreType.DMA
    hbm = functools.partial(pltpu.with_memory_space_constraint, memory_space=pltpu.HBM)
    east, west = pl.pallas_call(
        functools.partial(sweeps, rows, cols),
        out_shape=[jax.ShapeDtypeStruct(cut, jnp.bfloat16)] * 2,
        in_specs=[pl.BlockSpec(memory_space=pltpu.HBM)] * 3,
        out_specs=[pl.BlockSpec(memory_space=pltpu.VMEM)] * 2,
        scratch_shapes=[
            pltpu.VMEM((2, full // CHUNK, CHUNK, full), jnp.bfloat16),
            pltpu.VMEM((PIECES, blocks, block_rows, piece), jnp.bfloat16),
            trace,
            pltpu.VMEM((3, *cells), jnp.bfloat16),
            trace,
            pltpu.VMEM((block_rows, full), jnp.float32),
            pltpu.VMEM((block_rows, piece), jnp.bfloat16),
            dma((full // CHUNK,)), dma((PIECES,)),
            dma((blocks, PIECES)), dma((3, blocks, PIECES)),
            dma((1,)), dma((6,)), dma((2,)),
        ],
        compiler_params=pltpu.CompilerParams(
            collective_id=0, has_side_effects=True, vmem_limit_bytes=32 * 2**20),
        name="sweeps",
    )(hbm(matrix), hbm(east_sources.reshape(cut)), hbm(west_sources.reshape(cut)))
    anywhere = pl.BlockSpec(memory_space=pl.ANY)
    east, west = pl.pallas_call(
        flush,
        out_shape=[jax.ShapeDtypeStruct(cut, jnp.bfloat16)] * 2,
        in_specs=[anywhere] * 2,
        out_specs=[anywhere] * 2,
        scratch_shapes=[dma((2,))],
        compiler_params=pltpu.CompilerParams(vmem_limit_bytes=2**20),
        name="flush",
    )(east, west)
    return east.reshape(1, 1, batch, width), west.reshape(1, 1, batch, width)


def solution(mesh):
    in_specs = (
        P("crow", "ccol", "half", None),
        P("crow", "ccol", None, "half"),
        P("crow", "ccol", None, "half"),
    )
    out_specs = (P("crow", "ccol", None, "half"), P("crow", "ccol", None, "half"))
    body = functools.partial(local, mesh.shape["crow"], mesh.shape["ccol"])
    return jax.shard_map(body, mesh=mesh, in_specs=in_specs, out_specs=out_specs, check_vma=False)
```

time: 77.8 us -> 71.5 us (0.919)
  Pallas kernels: 75.2 us -> 70.4 us
  local copies, waits for them, and re-layouts: 1.76 us -> 0 us
    pallas_call x1, Pallas kernels: 75.2 us -> 69.2 us  [local(): pl.pallas_call(functools.partial(sweeps, rows, cols), out_shape=[jax.Shap...]
    unnamed x2 -> x0, local copies, waits for them, and re-layouts: 1.76 us -> none
    pallas_call x0 -> x1, Pallas kernels: none -> 1.16 us  [local(): pl.pallas_call(flush, out_shape=[jax.ShapeDtypeStruct(cut, jnp.bfloat16)]...]
where the time goes in v1:
time: 71.5 us; the launch traced here: 71 us
  Pallas kernels  70.4 us (98%)
    pallas_call x1, Pallas kernels, local(): pl.pallas_call(functools.partial(sweeps, rows, cols), out_shape=[jax.Shap...  69.2 us

profile of v1, /device:TPU:0, one launch (start us, length us, event | category | flops | bytes accessed | tf_op | source)
XLA Modules:
  0.0 71.0 jit_solution(15861195640532725617)
XLA Ops:
  0.6 69.2 %sweeps.1 = (bf16[12,32,1024]{2,1,0:T(8,128)(2,1)S(1)}, bf16[12,32,1024]{2,1,0:T(8,128)(2,1)S(1)}) custom-call(bf16[1024,2048]{1,0:T(8,128)(2,1)} %bitcast.5, bf16[12,32,1024]{2,1,0:T(8,128)(2,1)} %bitcast.6, bf16[12,32,1024]{2,1,0:T(8,128)(2,1)} %bitcast.7), custom_call_target="tpu_custom_call" | custom-call | tf_op jit(solution)/shard_map/sweeps/pallas_call | solution.py:369
  69.9 1.2 %flush.1 = (bf16[12,32,1024]{2,1,0:T(8,128)(2,1)}, bf16[12,32,1024]{2,1,0:T(8,128)(2,1)}) custom-call(bf16[12,32,1024]{2,1,0:T(8,128)(2,1)S(1)} %get-tuple-element.6.east, bf16[12,32,1024]{2,1,0:T(8,128)(2,1)S(1)} %get-tuple-element.7.west), custom_call_target="tpu_custom_call" | custom-call | tf_op jit(solution)/shard_map/flush/pallas_call | solution.py:391
